TPU v7x, 512 devices: a whole 4x4x16 slice. The times are simulated.
512 devices in a mesh: gy: 16 (over x_hi, y, core), gx: 32 (over z, x_lo).
Axes of the slice: x: 4 (x_hi: 2, x_lo: 2; x = x_hi * 2 + x_lo), y: 4, z: 16, core: 2. Of those that a mesh axis runs over, the one named last changes fastest.
Arguments:
- embeddings: bfloat16 [128, 4096, 128], P('gy', 'gx'), may hold values from -180 to 180
- affinity: float32 [4, 128, 4096], P(None, 'gy', 'gx'), may hold values from 0 to 1, as said below
- assignment: int32 [128, 4096], P('gy', 'gx'), may hold values from 0 to 1023
Outputs:
- min_distance: float32 [128, 4096], P('gy', 'gx')
- new_centroids: float32 [1024, 128], replicated
Inputs may be any that keep to these rules, and one draw needn't show every extreme that they name: `affinity`: weight 0 exactly for edges that leave the slab; every other edge weighs 0.05 or more.
All inputs are finite; a program needn't handle non-finite values.
Results may differ from a plain program's by a relative error of at most 0.00045.
Values may be sent and summed in bfloat16 or wider, within the bound.
No kernel may reach another device: no remote copies, remote signals or barrier semaphores. Data moves between devices by JAX's collectives and lax.ppermute only.
A program may use at most 64 MiB of HBM per device.

v0:
```python
import math
import jax
import jax.numpy as jnp
from jax import lax
from jax.sharding import PartitionSpec as P

K = 1024
DEGREE = 4
COEFFS = (0.5, 0.45, 0.35, 0.25, 0.15)


def extended(block, sides, width):
    for axis, dim in sides:
        count = lax.axis_size(axis)
        forward = [(i, i + 1) for i in range(count - 1)]
        backward = [(target, source) for source, target in forward]
        low = lax.ppermute(
            lax.slice_in_dim(block, block.shape[dim] - width, None, axis=dim), axis, forward
        )
        high = lax.ppermute(lax.slice_in_dim(block, 0, width, axis=dim), axis, backward)
        block = jnp.concatenate([low, block, high], axis=dim)
    return block


def degree_of(w_ext):
    w_east, w_south, w_diag, w_anti = (w_ext[0], w_ext[1], w_ext[2], w_ext[3])
    result = w_east[1:-1, 1:-1] + w_east[1:-1, :-2]
    result = result + w_south[1:-1, 1:-1] + w_south[:-2, 1:-1]
    result = result + w_diag[1:-1, 1:-1] + w_diag[:-2, :-2]
    return result + w_anti[1:-1, 1:-1] + w_anti[:-2, 2:]


def edge_sum(w_ext, field):
    w_east, w_south, w_diag, w_anti = (w_ext[0], w_ext[1], w_ext[2], w_ext[3])
    result = w_east[1:-1, 1:-1, None] * field[1:-1, 2:]
    result = result + w_east[1:-1, :-2, None] * field[1:-1, :-2]
    result = result + w_south[1:-1, 1:-1, None] * field[2:, 1:-1]
    result = result + w_south[:-2, 1:-1, None] * field[:-2, 1:-1]
    result = result + w_diag[1:-1, 1:-1, None] * field[2:, 2:]
    result = result + w_diag[:-2, :-2, None] * field[:-2, :-2]
    result = result + w_anti[1:-1, 1:-1, None] * field[2:, :-2]
    return result + w_anti[:-2, 2:, None] * field[:-2, 2:]


def whitening(gram, count):
    lower = jnp.linalg.cholesky(gram)
    identity = jnp.eye(gram.shape[0], dtype=gram.dtype)
    inverse = jax.scipy.linalg.solve_triangular(lower, identity, lower=True)
    return math.sqrt(count) * inverse.T


def on_device(embeddings, affinity, assignment):
    rows, cols, chans = embeddings.shape
    reach_all = DEGREE
    w_width = 1
    w_ext = extended(affinity, (("gy", 1), ("gx", 2)), w_width)
    scale = lax.rsqrt(degree_of(w_ext))[..., None]

    def apply_each(field):
        padded = extended(scale * field, (("gy", 0), ("gx", 1)), 1)
        return scale * edge_sum(w_ext, padded)

    previous = embeddings.astype(jnp.float32)
    current = apply_each(previous)
    filtered = COEFFS[0] * previous + COEFFS[1] * current
    for order in range(2, reach_all + 1):
        following = 2.0 * apply_each(current) - previous
        previous, current = (current, following)
        filtered = filtered + COEFFS[order] * following
    pixels = rows * cols
    flat = filtered.reshape(pixels, chans)
    labels = assignment.reshape(pixels)
    total_pixels = pixels * lax.axis_size("gy") * lax.axis_size("gx")
    clusters = K
    block = 128
    highest = lax.Precision.HIGHEST
    gram_local = lax.dot_general(
        flat, flat, (((0,), (0,)), ((), ())), precision=highest, preferred_element_type=jnp.float32
    )
    gram = lax.psum(gram_local, ("gy", "gx"))
    transform = whitening(gram, total_pixels)
    whitened = jnp.dot(flat, transform, precision=highest, preferred_element_type=jnp.float32)

    def one_block(index):
        first = index * block
        onehot = (labels[:, None] == first + jnp.arange(block, dtype=jnp.int32)[None, :]).astype(
            jnp.float32
        )
        partial_sums = lax.dot_general(
            onehot,
            whitened,
            (((0,), (0,)), ((), ())),
            precision=highest,
            preferred_element_type=jnp.float32,
        )
        return (partial_sums, jnp.sum(onehot, axis=0))

    block_sums, block_counts = lax.map(one_block, jnp.arange(clusters // block, dtype=jnp.int32))
    local_sums = block_sums.reshape(clusters, chans)
    local_counts = block_counts.reshape(clusters)
    sums, counts = lax.psum((local_sums, local_counts), ("gy", "gx"))
    centroids = sums / (counts + 1.0)[:, None]
    norms = jnp.sum(whitened * whitened, axis=1)

    def nearest(index, best):
        centre_part = lax.dynamic_slice_in_dim(centroids, index * block, block, 0)
        cross = lax.dot_general(
            whitened,
            centre_part,
            (((1,), (1,)), ((), ())),
            precision=highest,
            preferred_element_type=jnp.float32,
        )
        part_norms = jnp.sum(centre_part * centre_part, axis=1)
        distance = (norms[:, None] - 2.0 * cross + part_norms[None, :]) / chans
        return jnp.minimum(best, jnp.min(distance, axis=1))

    best = lax.fori_loop(0, clusters // block, nearest, jnp.full((pixels,), jnp.inf, jnp.float32))
    return (best.reshape(rows, cols), centroids)


def solution(mesh):
    return jax.shard_map(
        on_device,
        mesh=mesh,
        in_specs=(P("gy", "gx", None), P(None, "gy", "gx"), P("gy", "gx")),
        out_specs=(P("gy", "gx"), P()),
        check_vma=False,
    )
```

profile of v0, /device:TPU:4, one launch (start us, length us, event | category | flops | bytes accessed | tf_op | source)
XLA Modules:
  0.0 1084.3 jit_solution(14910961055857017236)
XLA Ops:
  8.0 2.0 collective-permute-start
  10.1 7.4 collective-permute-start.1
  19.6 3.1 collective-permute-start.2
  24.2 4.4 collective-permute-done.3
  29.1 1.9 collective-permute-start.4
  31.0 7.3 collective-permute-start.5
  38.3 1.9 collective-permute-done.5
  41.5 5.4 collective-permute-start.7
  48.3 1.7 broadcast_multiply_fusion.2
  50.1 1.9 collective-permute-start.8
  52.0 7.3 collective-permute-start.9
  59.3 1.9 collective-permute-done.9
  62.5 5.4 collective-permute-start.11
  69.3 1.7 broadcast_multiply_fusion.1
  71.0 1.9 collective-permute-start.12
  73.0 7.3 collective-permute-start.13
  80.2 1.9 collective-permute-done.13
  83.4 5.7 collective-permute-start.15
  90.6 1.7 broadcast_multiply_fusion
  92.3 1.9 collective-permute-start.16
  94.3 7.3 collective-permute-start.17
  101.5 1.9 collective-permute-done.17
  104.7 5.7 collective-permute-start.19
  111.9 1.7 fusion.14
  113.6 1.6 convolution_bitcast_fusion.1
  115.5 453.4 %all-reduce.3.cloned.1.call-done = f32[128,128]{0,1:T(8,128)} async-done(((f32[128,128]{0,1:T(8,128)}), f32[128,128]{0,1:T(8,128)}) %all-reduce.3.cloned.1.call-update) | async-done | bytes 65552 | tf_op jit(solution)/shard_map/psum | solution.py:80
  569.9 11.7 %cholesky.14 = f32[128,128]{1,0:T(8,128)S(1)} custom-call(f32[128,128]{1,0:T(8,128)S(1)} %fusion.63), custom_call_target="Cholesky" | custom-call | tf_op jit(solution)/shard_map/jit(cholesky)/cholesky | solution.py:46
  582.9 9.8 custom-call.7
  594.3 23.2 %while.26 = (s32[]{:T(128)}, f32[8,128,128]{2,1,0:T(8,128)}, f32[8,128]{1,0:T(8,128)S(1)}, s32[8,128]{1,0:T(8,128)S(1)}, s32[8]{0:T(128)S(1)}, /*index=5*/f32[10...) while((s32[]{:T(128)}, f32[8,128,128]{2,1,0:T(8,128)}, f32[8,128]{1,0:T(8,128)S(1)}, ...), condition=%wide.region_5.6_spmd, body=%wide.region_3.5_spmd.sunk | while | flops 201850880 | bytes 601725 | solution.py:98
  617.6 101.1 %psum.23 = f32[1024]{0:T(1024)S(1)} all-reduce(f32[1024]{0:T(1024)S(1)} %bitcast.54), channel_id=1, replica_groups=mesh['gy'=16,'gx'=32] {'gy','gx'}, use_global_device_ids=true, to_apply=%region_7.8 | all-reduce | flops 1024 | bytes 8192 | tf_op jit(solution)/shard_map/psum | solution.py:101
  718.7 350.4 %all-reduce.5.cloned.1.call-done = f32[1024,128]{1,0:T(8,128)} async-done(((f32[1024,128]{1,0:T(8,128)}), f32[1024,128]{1,0:T(8,128)}) %all-reduce.5.cloned.1.call-update) | async-done | bytes 524304 | tf_op jit(solution)/shard_map/psum | solution.py:101
  1070.3 6.3 while.27
  (133 shorter events, 45.8 us)
Async XLA Ops:
  7.2 561.7 %all-reduce.3.cloned.1.call-start = ((), (), s32[]{:S(2)}) async-start(), calls=%async_computation | async-start | bytes 131072 | tf_op jit(solution)/shard_map/psum | solution.py:80
  8.0 20.6 %copy-start.5 = (f32[4,8,128]{2,1,0:T(8,128)S(1)}, f32[4,8,128]{2,1,0:T(8,128)}, u32[]{:S(2)}) copy-start(f32[4,8,128]{2,1,0:T(8,128)} %param.8) | copy-start | bytes 49156
  8.0 9.5 collective-permute-start
  10.1 18.8 %copy-start = (bf16[8,128,128]{2,1,0:T(8,128)(2,1)S(1)}, bf16[8,128,128]{2,1,0:T(8,128)(2,1)}, u32[]{:S(2)}) copy-start(bf16[8,128,128]{2,1,0:T(8,128)(2,1)} %param.7) | copy-start | bytes 786436
  10.1 8.7 collective-permute-start.1
  19.6 4.7 collective-permute-start.2
  22.7 6.0 collective-permute-start.3
  29.1 9.2 collective-permute-start.4
  31.0 9.1 collective-permute-start.5
  40.2 6.8 collective-permute-start.6
  41.5 6.8 collective-permute-start.7
  50.1 9.2 collective-permute-start.8
  52.0 9.1 collective-permute-start.9
  61.2 6.8 collective-permute-start.10
  62.5 6.8 collective-permute-start.11
  71.0 9.2 collective-permute-start.12
  73.0 9.1 collective-permute-start.13
  82.1 7.0 collective-permute-start.14
  83.4 7.0 collective-permute-start.15
  92.3 9.2 collective-permute-start.16
  94.3 9.1 collective-permute-start.17
  103.4 7.0 collective-permute-start.18
  104.7 7.0 collective-permute-start.19
  115.2 953.8 %all-reduce.5.cloned.1.call-start = ((), (), s32[]{:S(2)}) async-start(), calls=%async_computation.1 | async-start | bytes 1048576 | tf_op jit(solution)/shard_map/psum | solution.py:101
  568.8 1.0 copy-start.3
  593.6 0.7 copy-start.2
  1076.6 0.8 copy-start.1
  1076.7 0.8 copy-start.4
Sparse Core Ops, SparseCore 0:
  115.3 453.4 all-reduce.2
  617.7 451.3 all-reduce.4
where the time goes:
time: 1090 us; the launch traced here: 1080 us
  waiting for transfers between devices  823 us (76%)
  blocking collectives  101 us (9%)
  starting transfers between devices  78.3 us (7%)
  other arithmetic  35.1 us (3%)
  matrix products  18.7 us (2%)
  between operations  14.5 us (1%)
    psum x1, waiting for transfers between devices, on_device(): gram = lax.psum(gram_local, ('gy', 'gx'))  453 us
    psum x1, waiting for transfers between devices, on_device(): sums, counts = lax.psum((local_sums, local_counts), ('gy', 'gx'))  350 us
    psum x1, blocking collectives, on_device(): sums, counts = lax.psum((local_sums, local_counts), ('gy', 'gx'))  101 us
    ppermute x10, starting transfers between devices, extended(): lax.ppermute(lax.slice_in_dim(block, 0, width, axis=dim), axis, backward)  42.9 us
    ppermute x10, starting transfers between devices, extended(): lax.ppermute(lax.slice_in_dim(block, block.shape[dim] - width, None, axis...  35.1 us
  transfers between devices with their start and end apart: 22, of which 13 were waited for; matrix products, arithmetic and copies ran while one was open for 0% of the time, Pallas kernels for 0%

commit v1 on v0

--- a/solution.py
+++ b/solution.py
@@ -50,6 +50,14 @@
 
 
 def on_device(embeddings, affinity, assignment):
+
+    def _shape_frame(my_data):
+        along_axis = "gy"
+        link_axis = "gx"
+        for ii in (link_axis, along_axis):
+            my_data = jax.lax.psum(my_data, ii)
+        return my_data
+
     rows, cols, chans = embeddings.shape
     reach_all = DEGREE
     w_width = 1
@@ -77,7 +85,7 @@
     gram_local = lax.dot_general(
         flat, flat, (((0,), (0,)), ((), ())), precision=highest, preferred_element_type=jnp.float32
     )
-    gram = lax.psum(gram_local, ("gy", "gx"))
+    gram = _shape_frame(gram_local)
     transform = whitening(gram, total_pixels)
     whitened = jnp.dot(flat, transform, precision=highest, preferred_element_type=jnp.float32)
 

time: 1090 us -> 1040 us (0.954)
  waiting for transfers between devices: 823 us -> 770 us
    psum x1 -> x2, waiting for transfers between devices: 453 us -> 397 us  [_shape_frame(): my_data = jax.lax.psum(my_data, ii)]
  transfers between devices with their start and end apart: 22 -> 23, of which waited for: 13 -> 14; matrix products, arithmetic and copies ran while one was open for 0% -> 0% of each run, Pallas kernels for 0% -> 0%
where the time goes in v1:
time: 1040 us
  waiting for transfers between devices  770 us (74%)
  blocking collectives  107 us (10%)
  starting transfers between devices  78.3 us (8%)
  other arithmetic  35.1 us (3%)
  matrix products  18.7 us (2%)
  between operations  14.2 us (1%)
    psum x2, waiting for transfers between devices, _shape_frame(): my_data = jax.lax.psum(my_data, ii)  397 us
    psum x1, waiting for transfers between devices, on_device(): sums, counts = lax.psum((local_sums, local_counts), ('gy', 'gx'))  355 us
    psum x1, blocking collectives, on_device(): sums, counts = lax.psum((local_sums, local_counts), ('gy', 'gx'))  107 us
    ppermute x10, starting transfers between devices, extended(): lax.ppermute(lax.slice_in_dim(block, 0, width, axis=dim), axis, backward)  42.9 us
    ppermute x10, starting transfers between devices, extended(): lax.ppermute(lax.slice_in_dim(block, block.shape[dim] - width, None, axis...  35.1 us
  transfers between devices with their start and end apart: 23, of which 14 were waited for; matrix products, arithmetic and copies ran while one was open for 0% of the time, Pallas kernels for 0%

profile of v1, /device:TPU:4, one launch (start us, length us, event | category | flops | bytes accessed | tf_op | source)
XLA Modules:
  0.0 1037.6 jit_solution(1300419834270484589)
XLA Ops:
  8.0 2.0 collective-permute-start
  10.1 7.4 collective-permute-start.1
  19.6 3.1 collective-permute-start.2
  24.2 4.4 collective-permute-done.3
  29.1 1.9 collective-permute-start.4
  31.0 7.3 collective-permute-start.5
  38.3 1.9 collective-permute-done.5
  41.5 5.4 collective-permute-start.7
  48.3 1.7 broadcast_multiply_fusion.2
  50.1 1.9 collective-permute-start.8
  52.0 7.3 collective-permute-start.9
  59.3 1.9 collective-permute-done.9
  62.5 5.4 collective-permute-start.11
  69.3 1.7 broadcast_multiply_fusion.1
  71.0 1.9 collective-permute-start.12
  73.0 7.3 collective-permute-start.13
  80.2 1.9 collective-permute-done.13
  83.4 5.7 collective-permute-start.15
  90.6 1.7 broadcast_multiply_fusion
  92.3 1.9 collective-permute-start.16
  94.3 7.3 collective-permute-start.17
  101.5 1.9 collective-permute-done.17
  104.7 5.7 collective-permute-start.19
  111.9 1.7 fusion.14
  115.3 260.2 %all-reduce.4.cloned.1.call-done = f32[128,128]{0,1:T(8,128)} async-done(((f32[128,128]{0,1:T(8,128)}), f32[128,128]{0,1:T(8,128)}) %all-reduce.4.cloned.1.call-update) | async-done | bytes 65552 | tf_op jit(solution)/shard_map/psum | solution.py:58
  375.8 136.4 %all-reduce.6.cloned.1.call-done = f32[128,128]{0,1:T(8,128)} async-done(((f32[128,128]{0,1:T(8,128)}), f32[128,128]{0,1:T(8,128)}) %all-reduce.6.cloned.1.call-update) | async-done | bytes 65552 | tf_op jit(solution)/shard_map/psum | solution.py:58
  513.1 11.7 %cholesky.14 = f32[128,128]{1,0:T(8,128)S(1)} custom-call(f32[128,128]{1,0:T(8,128)S(1)} %fusion.63), custom_call_target="Cholesky" | custom-call | tf_op jit(solution)/shard_map/jit(cholesky)/cholesky | solution.py:46
  526.2 9.8 custom-call.7
  537.6 23.2 %while.26 = (s32[]{:T(128)}, f32[8,128,128]{2,1,0:T(8,128)}, f32[8,128]{1,0:T(8,128)S(1)}, s32[8,128]{1,0:T(8,128)S(1)}, s32[8]{0:T(128)S(1)}, /*index=5*/f32[10...) while((s32[]{:T(128)}, f32[8,128,128]{2,1,0:T(8,128)}, f32[8,128]{1,0:T(8,128)S(1)}, ...), condition=%wide.region_6.7_spmd, body=%wide.region_4.6_spmd.sunk | while | flops 201850880 | bytes 601725 | solution.py:106
  560.8 107.0 %psum.31 = f32[1024]{0:T(1024)S(1)} all-reduce(f32[1024]{0:T(1024)S(1)} %bitcast.54), channel_id=1, replica_groups=mesh['gy'=16,'gx'=32] {'gy','gx'}, use_global_device_ids=true, to_apply=%region_8.9 | all-reduce | flops 1024 | bytes 8192 | tf_op jit(solution)/shard_map/psum | solution.py:109
  667.8 354.8 %all-reduce.8.cloned.1.call-done = f32[1024,128]{1,0:T(8,128)} async-done(((f32[1024,128]{1,0:T(8,128)}), f32[1024,128]{1,0:T(8,128)}) %all-reduce.8.cloned.1.call-update) | async-done | bytes 524304 | tf_op jit(solution)/shard_map/psum | solution.py:109
  1023.9 6.3 while.27
  (136 shorter events, 47.5 us)
Async XLA Ops:
  7.2 368.3 %all-reduce.4.cloned.1.call-start = ((), (), s32[]{:S(2)}) async-start(), calls=%async_computation | async-start | bytes 131072 | tf_op jit(solution)/shard_map/psum | solution.py:58
  8.0 20.6 %copy-start.5 = (f32[4,8,128]{2,1,0:T(8,128)S(1)}, f32[4,8,128]{2,1,0:T(8,128)}, u32[]{:S(2)}) copy-start(f32[4,8,128]{2,1,0:T(8,128)} %param.8) | copy-start | bytes 49156
  8.0 9.5 collective-permute-start
  10.1 18.8 %copy-start = (bf16[8,128,128]{2,1,0:T(8,128)(2,1)S(1)}, bf16[8,128,128]{2,1,0:T(8,128)(2,1)}, u32[]{:S(2)}) copy-start(bf16[8,128,128]{2,1,0:T(8,128)(2,1)} %param.7) | copy-start | bytes 786436
  10.1 8.7 collective-permute-start.1
  19.6 4.7 collective-permute-start.2
  22.7 6.0 collective-permute-start.3
  29.1 9.2 collective-permute-start.4
  31.0 9.1 collective-permute-start.5
  40.2 6.8 collective-permute-start.6
  41.5 6.8 collective-permute-start.7
  50.1 9.2 collective-permute-start.8
  52.0 9.1 collective-permute-start.9
  61.2 6.8 collective-permute-start.10
  62.5 6.8 collective-permute-start.11
  71.0 9.2 collective-permute-start.12
  73.0 9.1 collective-permute-start.13
  82.1 7.0 collective-permute-start.14
  83.4 7.0 collective-permute-start.15
  92.3 9.2 collective-permute-start.16
  94.3 9.1 collective-permute-start.17
  103.4 7.0 collective-permute-start.18
  104.7 7.0 collective-permute-start.19
  115.2 396.9 %all-reduce.6.cloned.1.call-start = ((), (), s32[]{:S(2)}) async-start(), calls=%async_computation.1 | async-start | bytes 131072 | tf_op jit(solution)/shard_map/psum | solution.py:58
  375.5 647.1 %all-reduce.8.cloned.1.call-start = ((), (), s32[]{:S(2)}) async-start(), calls=%async_computation.2 | async-start | bytes 1048576 | tf_op jit(solution)/shard_map/psum | solution.py:109
  512.1 1.0 copy-start.3
  536.9 0.7 copy-start.2
  1030.2 0.8 copy-start.1
  1030.3 0.8 copy-start.4
Sparse Core Ops, SparseCore 0:
  115.3 260.0 all-reduce.3
  378.7 133.4 all-reduce.5
  560.9 461.6 all-reduce.7
